TPU v7x, 256 devices: a whole 4x4x8 slice. The times are simulated.
256 devices in a mesh: seq: 32 (over y, x, core), chan: 8 (over z).
Axes of the slice: x: 4, y: 4, z: 8, core: 2. Of those that a mesh axis runs over, the one named last changes fastest.
Arguments:
- conv_in: bfloat16 [32, 512, 512], P(None, 'seq', 'chan'), may hold values from -4 to 4
- conv_gate: bfloat16 [32, 512, 512], P(None, 'seq', 'chan'), may hold values from -4 to 4
- long_filter: float32 [32, 512, 512], P(None, 'seq', 'chan'), may hold values from -1.1 to 1.1
- skip_gain: float32 [512], P('chan'), may hold values from 0.5 to 1.5
- queries: bfloat16 [32, 512, 1024], P(None, 'seq', 'chan'), may hold values from -40 to 40
- keys_in: bfloat16 [32, 512, 1024], P(None, 'seq', 'chan'), may hold values from -40 to 40
- w_value: bfloat16 [512, 1024], P(None, 'chan'), may hold values from -0.25 to 0.25
Outputs:
- conv_out: bfloat16 [32, 512, 512], P(None, 'seq', 'chan')
- attended: bfloat16 [32, 512, 1024], P(None, 'seq', 'chan')
All inputs are finite; a program needn't handle non-finite values.
Results may differ from a plain program's by a relative error of at most 0.015.
Values may be sent and summed in bfloat16 or wider, within the bound.
A program may use at most 64 MiB of HBM per device.

v0:
```python
import math
import jax
import jax.numpy as jnp
from jax import lax
from jax.sharding import PartitionSpec as P


def mixdot(form, left, right):
    return jnp.einsum(form, left, right, precision=lax.Precision.HIGHEST)


def channel_convolve(signal, long_filter):
    moved_sig, moved_tap = (
        lax.all_to_all(
            signal.astype(jnp.bfloat16), "seq", split_axis=2, concat_axis=1, tiled=True
        ).astype(signal.dtype),
        lax.all_to_all(
            long_filter.astype(jnp.bfloat16), "seq", split_axis=2, concat_axis=1, tiled=True
        ).astype(long_filter.dtype),
    )
    blocks = moved_sig.shape[0]
    length_q = moved_sig.shape[1]
    length_p = 2 * blocks
    total = length_p * length_q
    both = jnp.concatenate([moved_sig, moved_tap], axis=2).transpose(2, 0, 1)
    iota_p = jnp.arange(length_p, dtype=jnp.int32)
    iota_r = jnp.arange(blocks, dtype=jnp.int32)
    iota_q = jnp.arange(length_q, dtype=jnp.int32)
    ang_p = (iota_p[:, None] * iota_r[None, :] % length_p).astype(jnp.float32) * (
        2.0 * math.pi / length_p
    )
    ang_q = (iota_q[:, None] * iota_q[None, :] % length_q).astype(jnp.float32) * (
        2.0 * math.pi / length_q
    )
    ang_t = (iota_p[:, None] * iota_q[None, :] % total).astype(jnp.float32) * (
        2.0 * math.pi / total
    )
    cos_p = jnp.cos(ang_p)
    sin_p = jnp.sin(ang_p)
    cos_q = jnp.cos(ang_q)
    sin_q = jnp.sin(ang_q)
    cos_t = jnp.cos(ang_t)
    sin_t = jnp.sin(ang_t)
    first_re = mixdot("kn,cnq->ckq", cos_p, both)
    first_im = -mixdot("kn,cnq->ckq", sin_p, both)
    tw_re = first_re * cos_t + first_im * sin_t
    tw_im = first_im * cos_t - first_re * sin_t
    spec_re = mixdot("ckq,qm->ckm", tw_re, cos_q) + mixdot("ckq,qm->ckm", tw_im, sin_q)
    spec_im = mixdot("ckq,qm->ckm", tw_im, cos_q) - mixdot("ckq,qm->ckm", tw_re, sin_q)
    half_count = both.shape[0] // 2
    sig_re = spec_re[:half_count]
    sig_im = spec_im[:half_count]
    tap_re = spec_re[half_count:]
    tap_im = spec_im[half_count:]
    prod_re = sig_re * tap_re - sig_im * tap_im
    prod_im = sig_re * tap_im + sig_im * tap_re
    inner_re = mixdot("ckm,mq->ckq", prod_re, cos_q) - mixdot("ckm,mq->ckq", prod_im, sin_q)
    inner_im = mixdot("ckm,mq->ckq", prod_im, cos_q) + mixdot("ckm,mq->ckq", prod_re, sin_q)
    turned_re = inner_re * cos_t - inner_im * sin_t
    turned_im = inner_im * cos_t + inner_re * sin_t
    result = (mixdot("kn,ckq->cnq", cos_p, turned_re) - mixdot("kn,ckq->cnq", sin_p, turned_im)) * (
        1.0 / total
    )
    return lax.all_to_all(
        result.transpose(1, 2, 0).astype(jnp.bfloat16),
        "seq",
        split_axis=1,
        concat_axis=2,
        tiled=True,
    ).astype(jnp.float32)


def body(conv_in, conv_gate, long_filter, skip_gain, queries, keys_in, w_value):
    blocks, slab_rows, channels = conv_in.shape
    my_index = lax.axis_index("seq")
    tokens = blocks * slab_rows
    signal = conv_in.astype(jnp.float32)
    positions = (
        jnp.arange(blocks, dtype=jnp.int32)[:, None] * tokens
        + my_index * slab_rows
        + jnp.arange(slab_rows, dtype=jnp.int32)[None, :]
    )
    convolved = channel_convolve(signal, long_filter)
    mixed = (convolved + skip_gain * signal) * conv_gate.astype(jnp.float32)
    conv_out = mixed.astype(jnp.bfloat16)
    head_size = w_value.shape[1]
    piece = lax.all_gather(conv_out, "chan", axis=2, tiled=True)
    piece_width = piece.shape[2]
    value_sum = jnp.dot(
        piece.reshape(tokens, piece_width), w_value, preferred_element_type=jnp.float32
    )
    values = value_sum.astype(jnp.bfloat16).reshape(blocks, slab_rows, head_size)
    query_rows = queries.reshape(tokens, head_size)
    query_pos = positions.reshape(tokens)
    score_scale = 1.0 / math.sqrt(head_size)
    empty_state = (
        jnp.full((tokens,), -1e30, jnp.float32),
        jnp.zeros((tokens,), jnp.float32),
        jnp.zeros((tokens, head_size), jnp.float32),
    )
    key_piece = lax.all_gather(keys_in, "seq", axis=1, tiled=True)
    value_piece = lax.all_gather(values, "seq", axis=1, tiled=True)
    width_now = key_piece.shape[1]
    target = max(1, 1024 // blocks)
    step_size = 1
    for candidate in range(min(width_now, target), 0, -1):
        step_size = candidate
        break

    def key_step(step_index, current):
        row_best, row_total, row_accum = current
        offset = step_index * step_size
        key_block = lax.dynamic_slice_in_dim(key_piece, offset, step_size, 1).reshape(
            blocks * step_size, head_size
        )
        value_block = lax.dynamic_slice_in_dim(value_piece, offset, step_size, 1).reshape(
            blocks * step_size, head_size
        )
        key_pos = (
            jnp.arange(blocks, dtype=jnp.int32)[:, None] * tokens
            + offset
            + jnp.arange(step_size, dtype=jnp.int32)[None, :]
        ).reshape(blocks * step_size)
        scores = (
            jnp.einsum("qd,kd->qk", query_rows, key_block, preferred_element_type=jnp.float32)
            * score_scale
        )
        allowed = key_pos[None, :] <= query_pos[:, None]
        scores = jnp.where(allowed, scores, -1e30)
        new_best = jnp.maximum(row_best, jnp.max(scores, axis=1))
        factor = jnp.exp(row_best - new_best)
        weights = jnp.where(allowed, jnp.exp(scores - new_best[:, None]), 0.0)
        row_total = row_total * factor + jnp.sum(weights, axis=1)
        row_accum = row_accum * factor[:, None] + jnp.dot(
            weights.astype(jnp.bfloat16), value_block, preferred_element_type=jnp.float32
        )
        return (new_best, row_total, row_accum)

    final_best, final_total, final_accum = lax.fori_loop(
        0, width_now // step_size, key_step, empty_state
    )
    attended = (
        (final_accum / final_total[:, None])
        .astype(jnp.bfloat16)
        .reshape(blocks, slab_rows, head_size)
    )
    return (conv_out, attended)


def solution(mesh):
    return jax.shard_map(
        body,
        mesh=mesh,
        in_specs=(
            P(None, "seq", "chan"),
            P(None, "seq", "chan"),
            P(None, "seq", "chan"),
            P("chan"),
            P(None, "seq", "chan"),
            P(None, "seq", "chan"),
            P(None, "chan"),
        ),
        out_specs=(P(None, "seq", "chan"), P(None, "seq", "chan")),
        check_vma=False,
    )
```

profile of v0, /device:TPU:1, one launch (start us, length us, event | category | flops | bytes accessed | tf_op | source)
XLA Modules:
  0.0 245.0 jit_solution(10891590349229744156)
XLA Ops:
  10.0 8.6 %all-to-all-start.1 = ((bf16[32,2,512]{2,1,0:T(2,128)(2,1)}), bf16[32,2,512]{2,1,0:T(2,128)(2,1)S(1)}, u32[]{:S(2)}, u32[]{:S(2)}) async-start(bf16[32,2,512]{2,1,0:T(2,128)(2,1)} %reshape.130), calls=%async_computation.1 | async-start | bytes 131072 | tf_op jit(solution)/shard_map/all_to_all | solution.py:17
  18.6 1.2 copy.75
  20.7 5.2 %all-to-all-done.1 = bf16[32,2,512]{2,1,0:T(2,128)(2,1)S(1)} async-done(((bf16[32,2,512]{2,1,0:T(2,128)(2,1)}), bf16[32,2,512]{2,1,0:T(2,128)(2,1)S(1)}, u32[]{:S(2)}, u32[]{:S(2)}) %all-to-all-start.1) | async-done | bytes 65568 | tf_op jit(solution)/shard_map/all_to_all | solution.py:17
  26.0 3.9 %all-to-all-start = ((bf16[32,2,512]{2,1,0:T(2,128)(2,1)}), bf16[32,2,512]{2,1,0:T(2,128)(2,1)S(1)}, u32[]{:S(2)}, u32[]{:S(2)}) async-start(bf16[32,2,512]{2,1,0:T(2,128)(2,1)} %reshape.132), calls=%async_computation | async-start | bytes 131072 | tf_op jit(solution)/shard_map/all_to_all | solution.py:14
  30.7 6.6 %all-to-all-done = bf16[32,2,512]{2,1,0:T(2,128)(2,1)S(1)} async-done(((bf16[32,2,512]{2,1,0:T(2,128)(2,1)}), bf16[32,2,512]{2,1,0:T(2,128)(2,1)S(1)}, u32[]{:S(2)}, u32[]{:S(2)}) %all-to-all-start) | async-done | bytes 65568 | tf_op jit(solution)/shard_map/all_to_all | solution.py:14
  38.7 5.4 %fusion.30 = f32[4,64,512]{2,1,0:T(8,128)S(1)} fusion(f32[4,64,512]{2,1,0:T(8,128)S(1)} %convolution_bitcast_fusion, f32[4,64,512]{2,1,0:T(8,128)S(1)} %fusion.15, f32[64,512]{1,0:T(8,128)S(1)} %get-tuple-element.210, f32[64,512]{1,0:T(8,128)S(1)} %get-tuple-element.211), kind=kOutput, calls=%fused_computation.51 | convolution fusion | flops 809369600 | bytes 1835008 | tf_op jit(solution)/shard_map/ckq,qm->ckm/dot_general | solution.py:9
  44.1 5.4 %fusion.32 = f32[4,64,512]{2,1,0:T(8,128)S(1)} fusion(f32[4,64,512]{2,1,0:T(8,128)S(1)} %fusion.15, f32[4,64,512]{2,1,0:T(8,128)S(1)} %convolution_bitcast_fusion, f32[64,512]{1,0:T(8,128)S(1)} %get-tuple-element.210, f32[64,512]{1,0:T(8,128)S(1)} %get-tuple-element.211), kind=kOutput, calls=%fused_computation.53 | convolution fusion | flops 809369600 | bytes 1835008 | tf_op jit(solution)/shard_map/ckq,qm->ckm/dot_general | solution.py:9
  49.5 5.4 %convolution_subtract_fusion = f32[4,64,512]{2,1,0:T(8,128)S(1)} fusion(f32[4,64,512]{2,1,0:T(8,128)S(1)} %fusion.30, f32[4,64,512]{2,1,0:T(8,128)S(1)} %fusion.15, f32[4,64,512]{2,1,0:T(8,128)S(1)} %convolution_bitcast_fusion, f32[64,512]{1,0:T(8,128)S(1)} %get-tuple-element.210, f32[64,512]{1,0:T(8,128)S(1)} %get-tuple-element.211), kind=kOutput, calls=%fused_computation.28 | convolution fusion | flops 809500672 | bytes 2359296 | tf_op jit(solution)/shard_map/ckq,qm->ckm/dot_general | solution.py:9
  54.9 5.6 %convolution_add_fusion.1 = f32[4,64,512]{2,1,0:T(8,128)S(1)} fusion(f32[4,64,512]{2,1,0:T(8,128)S(1)} %fusion.32, f32[4,64,512]{2,1,0:T(8,128)S(1)} %convolution_bitcast_fusion, f32[4,64,512]{2,1,0:T(8,128)S(1)} %fusion.15, f32[64,512]{1,0:T(8,128)S(1)} %get-tuple-element.210, f32[64,512]{1,0:T(8,128)S(1)} %get-tuple-element.211), kind=kOutput, calls=%fused_computation.29 | convolution fusion | flops 809500672 | bytes 2359296 | tf_op jit(solution)/shard_map/ckq,qm->ckm/dot_general | solution.py:9
  60.6 4.9 %fusion.28 = f32[2,64,512]{2,1,0:T(8,128)S(1)} fusion(f32[2,64,512]{2,1,0:T(8,128)S(1)} %get-tuple-element.208), kind=kOutput, calls=%fused_computation.49 | convolution fusion | flops 406323200 | bytes 524288 | tf_op jit(solution)/shard_map/ckm,mq->ckq/dot_general | solution.py:9
  65.5 4.9 %fusion.26 = f32[2,64,512]{2,1,0:T(8,128)S(1)} fusion(f32[2,64,512]{2,1,0:T(8,128)S(1)} %get-tuple-element.209), kind=kOutput, calls=%fused_computation.47 | convolution fusion | flops 406323200 | bytes 524288 | tf_op jit(solution)/shard_map/ckm,mq->ckq/dot_general | solution.py:9
  70.4 4.9 %convolution_subtract_fusion.1 = f32[2,64,512]{2,1,0:T(8,128)S(1)} fusion(f32[2,64,512]{2,1,0:T(8,128)S(1)} %fusion.28, f32[2,64,512]{2,1,0:T(8,128)S(1)} %get-tuple-element.209), kind=kOutput, calls=%fused_computation.34 | convolution fusion | flops 406388736 | bytes 786432 | tf_op jit(solution)/shard_map/ckm,mq->ckq/dot_general | solution.py:9
  75.2 5.1 %convolution_add_fusion.2 = f32[2,64,512]{2,1,0:T(8,128)S(1)} fusion(f32[2,64,512]{2,1,0:T(8,128)S(1)} %fusion.26, f32[2,64,512]{2,1,0:T(8,128)S(1)} %get-tuple-element.208), kind=kOutput, calls=%fused_computation.33 | convolution fusion | flops 406388736 | bytes 786432 | tf_op jit(solution)/shard_map/ckm,mq->ckq/dot_general | solution.py:9
  82.2 3.9 %all-to-all-start.2 = ((bf16[32,2,512]{2,1,0:T(2,128)(2,1)}), bf16[32,2,512]{2,1,0:T(2,128)(2,1)S(1)}, u32[]{:S(2)}, u32[]{:S(2)}) async-start(bf16[32,2,512]{2,1,0:T(2,128)(2,1)} %reshape.134), calls=%async_computation.2 | async-start | bytes 131072 | tf_op jit(solution)/shard_map/all_to_all | solution.py:64
  86.5 7.1 %all-to-all-done.2 = bf16[32,2,512]{2,1,0:T(2,128)(2,1)S(1)} async-done(((bf16[32,2,512]{2,1,0:T(2,128)(2,1)}), bf16[32,2,512]{2,1,0:T(2,128)(2,1)S(1)}, u32[]{:S(2)}, u32[]{:S(2)}) %all-to-all-start.2) | async-done | bytes 65568 | tf_op jit(solution)/shard_map/all_to_all | solution.py:64
  94.1 28.8 %all_gather.10 = bf16[32,16,512]{0,1,2:T(8,128)(2,1)S(1)} all-gather(bf16[32,16,64]{0,1,2:T(8,128)(2,1)S(1)} %fusion.38), channel_id=1, replica_groups=mesh['seq'=32,'chan'=8] {'chan'}, dimensions={2}, use_global_device_ids=true | all-gather | bytes 589824 | tf_op jit(solution)/shard_map/all_gather | solution.py:87
  123.0 2.2 copy.86
  127.2 53.7 %all-gather.5.cloned.1.call-done = bf16[32,512,128]{2,1,0:T(8,128)(2,1)} async-done(((bf16[32,16,128]{2,1,0:T(8,128)(2,1)}), bf16[32,512,128]{2,1,0:T(8,128)(2,1)}) %all-gather.5.cloned.1.call-update) | async-done | bytes 4194320 | tf_op jit(solution)/shard_map/all_gather | solution.py:102
  180.8 56.5 %while.18 = (s32[]{:T(128)}, f32[512]{0:T(512)S(1)}, f32[512]{0:T(512)S(1)}, f32[512,128]{1,0:T(8,128)S(1)}, bf16[32,512,128]{2,1,0:T(8,128)(2,1)}, /*index=5*/b...) while((s32[]{:T(128)}, f32[512]{0:T(512)S(1)}, ...), condition=%wide.region_3.4_spmd.clone, body=%wide.region_0.3_spmd.clone.sunk | while | flops 277024832 | bytes 8589887 | solution.py:139
  184.7 1.1 constant_dynamic-slice_fusion.3
  191.7 1.1 constant_dynamic-slice_fusion.3
  198.8 1.1 constant_dynamic-slice_fusion.3
  209.4 1.1 constant_dynamic-slice_fusion.3
  216.4 1.1 constant_dynamic-slice_fusion.3
  (231 shorter events, 61.5 us)
Async XLA Ops:
  7.2 118.0 %copy-start = (bf16[512,128]{1,0:T(8,128)(2,1)S(1)}, bf16[512,128]{1,0:T(8,128)(2,1)}, u32[]{:S(2)}) copy-start(bf16[512,128]{1,0:T(8,128)(2,1)} %param.15) | copy-start | bytes 393220
  7.2 120.0 %all-gather.3.cloned.1.call-start = ((), (), s32[]{:S(2)}) async-start(), calls=%async_computation.3 | async-start | bytes 4325376 | tf_op jit(solution)/shard_map/all_gather | solution.py:101
  10.0 15.9 %all-to-all-start.1 = ((bf16[32,2,512]{2,1,0:T(2,128)(2,1)}), bf16[32,2,512]{2,1,0:T(2,128)(2,1)S(1)}, u32[]{:S(2)}, u32[]{:S(2)}) async-start(bf16[32,2,512]{2,1,0:T(2,128)(2,1)} %reshape.130), calls=%async_computation.1 | async-start | bytes 131072 | tf_op jit(solution)/shard_map/all_to_all | solution.py:17
  26.0 11.3 %all-to-all-start = ((bf16[32,2,512]{2,1,0:T(2,128)(2,1)}), bf16[32,2,512]{2,1,0:T(2,128)(2,1)S(1)}, u32[]{:S(2)}, u32[]{:S(2)}) async-start(bf16[32,2,512]{2,1,0:T(2,128)(2,1)} %reshape.132), calls=%async_computation | async-start | bytes 131072 | tf_op jit(solution)/shard_map/all_to_all | solution.py:14
  80.3 5.9 %copy-start.1 = (bf16[32,16,64]{2,1,0:T(8,128)(2,1)S(1)}, bf16[32,16,64]{2,1,0:T(8,128)(2,1)}, u32[]{:S(2)}) copy-start(bf16[32,16,64]{2,1,0:T(8,128)(2,1)} %param.10) | copy-start | bytes 196612
  81.2 12.8 %copy-start.2 = (f32[64]{0:T(128)S(1)}, f32[64]{0:T(128)}, u32[]{:S(2)}) copy-start(f32[64]{0:T(128)} %param.12) | copy-start | bytes 772
  82.2 11.4 %all-to-all-start.2 = ((bf16[32,2,512]{2,1,0:T(2,128)(2,1)}), bf16[32,2,512]{2,1,0:T(2,128)(2,1)S(1)}, u32[]{:S(2)}, u32[]{:S(2)}) async-start(bf16[32,2,512]{2,1,0:T(2,128)(2,1)} %reshape.134), calls=%async_computation.2 | async-start | bytes 131072 | tf_op jit(solution)/shard_map/all_to_all | solution.py:64
  86.2 94.6 %all-gather.5.cloned.1.call-start = ((), (), s32[]{:S(2)}) async-start(), calls=%async_computation.4 | async-start | bytes 4325376 | tf_op jit(solution)/shard_map/all_gather | solution.py:102
  123.0 57.8 %copy-start.3 = (bf16[32,16,128]{2,1,0:T(8,128)(2,1)S(1)}, bf16[32,16,128]{2,1,0:T(8,128)(2,1)}, u32[]{:S(2)}) copy-start(bf16[32,16,128]{2,1,0:T(8,128)(2,1)} %param.13) | copy-start | bytes 393220
Sparse Core Ops, SparseCore 0:
  10.5 58.7 all-gather.2
  126.3 54.5 all-gather.4
where the time goes:
time: 246 us; the launch traced here: 245 us
  waiting for transfers between devices  73.2 us (30%)
  matrix products  67.3 us (27%)
  blocking collectives  28.8 us (12%)
  local copies, waits for them, and re-layouts  28.4 us (12%)
  starting transfers between devices  16.5 us (7%)
  other arithmetic  15.3 us (6%)
  between operations  14.4 us (6%)
    all_gather x1, waiting for transfers between devices, body(): value_piece = lax.all_gather(values, 'seq', axis=1, tiled=True)  53.7 us
    dot_general x12, matrix products, mixdot(): return jnp.einsum(form, left, right, precision=lax.Precision.HIGHEST)  43.3 us
    all_gather x1, blocking collectives, body(): piece = lax.all_gather(conv_out, 'chan', axis=2, tiled=True)  28.8 us
    dynamic_slice x16, local copies, waits for them, and re-layouts, key_step(): lax.dynamic_slice_in_dim(value_piece, offset, step_size, 1)  17.2 us
    dot_general x16, matrix products, key_step(): jnp.dot(weights.astype(jnp.bfloat16), value_block, preferred_element_type...  15.7 us
    reduce_sum x16, other arithmetic, key_step(): row_total = row_total * factor + jnp.sum(weights, axis=1)  9.97 us
    all_to_all x1, starting transfers between devices, channel_convolve(): lax.all_to_all(long_filter.astype(jnp.bfloat16), 'seq', split_axis=2, con...  8.59 us
    dot_general x16, matrix products, key_step(): jnp.einsum('qd,kd->qk', query_rows, key_block, preferred_element_type=jnp...  7.38 us
  transfers between devices with their start and end apart: 5, of which 4 were waited for; matrix products, arithmetic and copies ran while one was open for 22% of the time, Pallas kernels for 0%

commit v1 on v0

--- a/solution.py
+++ b/solution.py
@@ -84,7 +84,9 @@
     mixed = (convolved + skip_gain * signal) * conv_gate.astype(jnp.float32)
     conv_out = mixed.astype(jnp.bfloat16)
     head_size = w_value.shape[1]
-    piece = lax.all_gather(conv_out, "chan", axis=2, tiled=True)
+    piece = jnp.concatenate(
+        lax.all_to_all(jnp.stack([conv_out] * lax.axis_size("chan")), "chan", 0, 0), axis=2
+    )
     piece_width = piece.shape[2]
     value_sum = jnp.dot(
         piece.reshape(tokens, piece_width), w_value, preferred_element_type=jnp.float32

time: 246 us -> 237 us (0.963)
  waiting for transfers between devices: 73.2 us -> 68 us
  blocking collectives: 28.8 us -> 24.6 us
    all_gather x1 -> x0, blocking collectives: 28.8 us -> none  [body(): piece = lax.all_gather(conv_out, 'chan', axis=2, tiled=True)]
    all_to_all x0 -> x1, blocking collectives: none -> 24.6 us  [body(): lax.all_to_all(jnp.stack([conv_out] * lax.axis_size('chan')), 'chan', 0, 0)]
    all_gather x1, waiting for transfers between devices: 53.7 us -> 48.4 us  [body(): value_piece = lax.all_gather(values, 'seq', axis=1, tiled=True)]
    unnamed x17 -> x21, local copies, waits for them, and re-layouts: 5.61 us -> 6.33 us
  transfers between devices with their start and end apart: 5 -> 5, of which waited for: 4 -> 4; matrix products, arithmetic and copies ran while one was open for 22% -> 23% of each run, Pallas kernels for 0% -> 0%
where the time goes in v1:
time: 237 us; the launch traced here: 236 us
  waiting for transfers between devices  68 us (29%)
  matrix products  67.3 us (28%)
  local copies, waits for them, and re-layouts  28.9 us (12%)
  blocking collectives  24.6 us (10%)
  starting transfers between devices  16.5 us (7%)
  other arithmetic  15.3 us (6%)
  between operations  14.4 us (6%)
    all_gather x1, waiting for transfers between devices, body(): value_piece = lax.all_gather(values, 'seq', axis=1, tiled=True)  48.4 us
    dot_general x12, matrix products, mixdot(): return jnp.einsum(form, left, right, precision=lax.Precision.HIGHEST)  43.3 us
    all_to_all x1, blocking collectives, body(): lax.all_to_all(jnp.stack([conv_out] * lax.axis_size('chan')), 'chan', 0, 0)  24.6 us
    dynamic_slice x16, local copies, waits for them, and re-layouts, key_step(): lax.dynamic_slice_in_dim(value_piece, offset, step_size, 1)  17.2 us
    dot_general x16, matrix products, key_step(): jnp.dot(weights.astype(jnp.bfloat16), value_block, preferred_element_type...  15.7 us
    reduce_sum x16, other arithmetic, key_step(): row_total = row_total * factor + jnp.sum(weights, axis=1)  9.97 us
    all_to_all x1, starting transfers between devices, channel_convolve(): lax.all_to_all(long_filter.astype(jnp.bfloat16), 'seq', split_axis=2, con...  8.59 us
    dot_general x16, matrix products, key_step(): jnp.einsum('qd,kd->qk', query_rows, key_block, preferred_element_type=jnp...  7.35 us
  transfers between devices with their start and end apart: 5, of which 4 were waited for; matrix products, arithmetic and copies ran while one was open for 23% of the time, Pallas kernels for 0%

profile of v1, /device:TPU:1, one launch (start us, length us, event | category | flops | bytes accessed | tf_op | source)
XLA Modules:
  0.0 236.0 jit_solution(656207928193739853)
XLA Ops:
  10.0 8.6 %all-to-all-start.1 = ((bf16[32,2,512]{2,1,0:T(2,128)(2,1)}), bf16[32,2,512]{2,1,0:T(2,128)(2,1)S(1)}, u32[]{:S(2)}, u32[]{:S(2)}) async-start(bf16[32,2,512]{2,1,0:T(2,128)(2,1)} %reshape.132), calls=%async_computation.1 | async-start | bytes 131072 | tf_op jit(solution)/shard_map/all_to_all | solution.py:17
  18.6 1.2 copy.67
  20.7 5.2 %all-to-all-done.1 = bf16[32,2,512]{2,1,0:T(2,128)(2,1)S(1)} async-done(((bf16[32,2,512]{2,1,0:T(2,128)(2,1)}), bf16[32,2,512]{2,1,0:T(2,128)(2,1)S(1)}, u32[]{:S(2)}, u32[]{:S(2)}) %all-to-all-start.1) | async-done | bytes 65568 | tf_op jit(solution)/shard_map/all_to_all | solution.py:17
  26.0 3.9 %all-to-all-start = ((bf16[32,2,512]{2,1,0:T(2,128)(2,1)}), bf16[32,2,512]{2,1,0:T(2,128)(2,1)S(1)}, u32[]{:S(2)}, u32[]{:S(2)}) async-start(bf16[32,2,512]{2,1,0:T(2,128)(2,1)} %reshape.134), calls=%async_computation | async-start | bytes 131072 | tf_op jit(solution)/shard_map/all_to_all | solution.py:14
  30.7 6.6 %all-to-all-done = bf16[32,2,512]{2,1,0:T(2,128)(2,1)S(1)} async-done(((bf16[32,2,512]{2,1,0:T(2,128)(2,1)}), bf16[32,2,512]{2,1,0:T(2,128)(2,1)S(1)}, u32[]{:S(2)}, u32[]{:S(2)}) %all-to-all-start) | async-done | bytes 65568 | tf_op jit(solution)/shard_map/all_to_all | solution.py:14
  38.7 5.4 %fusion.30 = f32[4,64,512]{2,1,0:T(8,128)S(1)} fusion(f32[4,64,512]{2,1,0:T(8,128)S(1)} %convolution_bitcast_fusion, f32[4,64,512]{2,1,0:T(8,128)S(1)} %fusion.15, f32[64,512]{1,0:T(8,128)S(1)} %get-tuple-element.208, f32[64,512]{1,0:T(8,128)S(1)} %get-tuple-element.209), kind=kOutput, calls=%fused_computation.51 | convolution fusion | flops 809369600 | bytes 1835008 | tf_op jit(solution)/shard_map/ckq,qm->ckm/dot_general | solution.py:9
  44.1 5.4 %fusion.32 = f32[4,64,512]{2,1,0:T(8,128)S(1)} fusion(f32[4,64,512]{2,1,0:T(8,128)S(1)} %fusion.15, f32[4,64,512]{2,1,0:T(8,128)S(1)} %convolution_bitcast_fusion, f32[64,512]{1,0:T(8,128)S(1)} %get-tuple-element.208, f32[64,512]{1,0:T(8,128)S(1)} %get-tuple-element.209), kind=kOutput, calls=%fused_computation.53 | convolution fusion | flops 809369600 | bytes 1835008 | tf_op jit(solution)/shard_map/ckq,qm->ckm/dot_general | solution.py:9
  49.5 5.4 %convolution_subtract_fusion = f32[4,64,512]{2,1,0:T(8,128)S(1)} fusion(f32[4,64,512]{2,1,0:T(8,128)S(1)} %fusion.30, f32[4,64,512]{2,1,0:T(8,128)S(1)} %fusion.15, f32[4,64,512]{2,1,0:T(8,128)S(1)} %convolution_bitcast_fusion, f32[64,512]{1,0:T(8,128)S(1)} %get-tuple-element.208, f32[64,512]{1,0:T(8,128)S(1)} %get-tuple-element.209), kind=kOutput, calls=%fused_computation.28 | convolution fusion | flops 809500672 | bytes 2359296 | tf_op jit(solution)/shard_map/ckq,qm->ckm/dot_general | solution.py:9
  54.9 5.6 %convolution_add_fusion.1 = f32[4,64,512]{2,1,0:T(8,128)S(1)} fusion(f32[4,64,512]{2,1,0:T(8,128)S(1)} %fusion.32, f32[4,64,512]{2,1,0:T(8,128)S(1)} %convolution_bitcast_fusion, f32[4,64,512]{2,1,0:T(8,128)S(1)} %fusion.15, f32[64,512]{1,0:T(8,128)S(1)} %get-tuple-element.208, f32[64,512]{1,0:T(8,128)S(1)} %get-tuple-element.209), kind=kOutput, calls=%fused_computation.29 | convolution fusion | flops 809500672 | bytes 2359296 | tf_op jit(solution)/shard_map/ckq,qm->ckm/dot_general | solution.py:9
  60.6 4.9 %fusion.28 = f32[2,64,512]{2,1,0:T(8,128)S(1)} fusion(f32[2,64,512]{2,1,0:T(8,128)S(1)} %get-tuple-element.206), kind=kOutput, calls=%fused_computation.49 | convolution fusion | flops 406323200 | bytes 524288 | tf_op jit(solution)/shard_map/ckm,mq->ckq/dot_general | solution.py:9
  65.5 4.9 %fusion.26 = f32[2,64,512]{2,1,0:T(8,128)S(1)} fusion(f32[2,64,512]{2,1,0:T(8,128)S(1)} %get-tuple-element.207), kind=kOutput, calls=%fused_computation.47 | convolution fusion | flops 406323200 | bytes 524288 | tf_op jit(solution)/shard_map/ckm,mq->ckq/dot_general | solution.py:9
  70.4 4.9 %convolution_subtract_fusion.1 = f32[2,64,512]{2,1,0:T(8,128)S(1)} fusion(f32[2,64,512]{2,1,0:T(8,128)S(1)} %fusion.28, f32[2,64,512]{2,1,0:T(8,128)S(1)} %get-tuple-element.207), kind=kOutput, calls=%fused_computation.34 | convolution fusion | flops 406388736 | bytes 786432 | tf_op jit(solution)/shard_map/ckm,mq->ckq/dot_general | solution.py:9
  75.2 5.1 %convolution_add_fusion.2 = f32[2,64,512]{2,1,0:T(8,128)S(1)} fusion(f32[2,64,512]{2,1,0:T(8,128)S(1)} %fusion.26, f32[2,64,512]{2,1,0:T(8,128)S(1)} %get-tuple-element.206), kind=kOutput, calls=%fused_computation.33 | convolution fusion | flops 406388736 | bytes 786432 | tf_op jit(solution)/shard_map/ckm,mq->ckq/dot_general | solution.py:9
  82.2 3.9 %all-to-all-start.2 = ((bf16[32,2,512]{2,1,0:T(2,128)(2,1)}), bf16[32,2,512]{2,1,0:T(2,128)(2,1)S(1)}, u32[]{:S(2)}, u32[]{:S(2)}) async-start(bf16[32,2,512]{2,1,0:T(2,128)(2,1)} %reshape.136), calls=%async_computation.2 | async-start | bytes 131072 | tf_op jit(solution)/shard_map/all_to_all | solution.py:64
  86.5 7.1 %all-to-all-done.2 = bf16[32,2,512]{2,1,0:T(2,128)(2,1)S(1)} async-done(((bf16[32,2,512]{2,1,0:T(2,128)(2,1)}), bf16[32,2,512]{2,1,0:T(2,128)(2,1)S(1)}, u32[]{:S(2)}, u32[]{:S(2)}) %all-to-all-start.2) | async-done | bytes 65568 | tf_op jit(solution)/shard_map/all_to_all | solution.py:64
  95.3 24.6 %all_to_all.32 = bf16[8,2,16384]{2,1,0:T(2,128)(2,1)S(1)} all-to-all(bf16[8,2,16384]{2,1,0:T(2,128)(2,1)S(1)} %reshape.138), channel_id=1, replica_groups=mesh['seq'=32,'chan'=8] {'chan'}, dimensions={0} | all-to-all | bytes 1048576 | tf_op jit(solution)/shard_map/all_to_all | solution.py:88
  120.6 1.2 copy.79
  123.5 48.4 %all-gather.5.cloned.1.call-done = bf16[32,512,128]{2,1,0:T(8,128)(2,1)} async-done(((bf16[32,16,128]{2,1,0:T(8,128)(2,1)}), bf16[32,512,128]{2,1,0:T(8,128)(2,1)}) %all-gather.5.cloned.1.call-update) | async-done | bytes 4194320 | tf_op jit(solution)/shard_map/all_gather | solution.py:104
  171.9 56.5 %while.18 = (s32[]{:T(128)}, f32[512]{0:T(512)S(1)}, f32[512]{0:T(512)S(1)}, f32[512,128]{1,0:T(8,128)S(1)}, bf16[32,512,128]{2,1,0:T(8,128)(2,1)}, /*index=5*/b...) while((s32[]{:T(128)}, f32[512]{0:T(512)S(1)}, ...), condition=%wide.region_3.4_spmd.clone, body=%wide.region_0.3_spmd.clone.sunk | while | flops 277024832 | bytes 8589887 | solution.py:141
  175.7 1.1 constant_dynamic-slice_fusion.3
  182.8 1.1 constant_dynamic-slice_fusion.3
  186.3 1.1 constant_dynamic-slice_fusion.3
  200.4 1.1 constant_dynamic-slice_fusion.3
  211.0 1.1 constant_dynamic-slice_fusion.3
  (237 shorter events, 63.0 us)
Async XLA Ops:
  7.2 115.2 %copy-start = (bf16[512,128]{1,0:T(8,128)(2,1)S(1)}, bf16[512,128]{1,0:T(8,128)(2,1)}, u32[]{:S(2)}) copy-start(bf16[512,128]{1,0:T(8,128)(2,1)} %param.15) | copy-start | bytes 393220
  7.2 116.3 %all-gather.3.cloned.1.call-start = ((), (), s32[]{:S(2)}) async-start(), calls=%async_computation.4 | async-start | bytes 4325376 | tf_op jit(solution)/shard_map/all_gather | solution.py:103
  10.0 15.9 %all-to-all-start.1 = ((bf16[32,2,512]{2,1,0:T(2,128)(2,1)}), bf16[32,2,512]{2,1,0:T(2,128)(2,1)S(1)}, u32[]{:S(2)}, u32[]{:S(2)}) async-start(bf16[32,2,512]{2,1,0:T(2,128)(2,1)} %reshape.132), calls=%async_computation.1 | async-start | bytes 131072 | tf_op jit(solution)/shard_map/all_to_all | solution.py:17
  26.0 11.3 %all-to-all-start = ((bf16[32,2,512]{2,1,0:T(2,128)(2,1)}), bf16[32,2,512]{2,1,0:T(2,128)(2,1)S(1)}, u32[]{:S(2)}, u32[]{:S(2)}) async-start(bf16[32,2,512]{2,1,0:T(2,128)(2,1)} %reshape.134), calls=%async_computation | async-start | bytes 131072 | tf_op jit(solution)/shard_map/all_to_all | solution.py:14
  80.3 5.9 %copy-start.2 = (bf16[32,16,64]{2,1,0:T(8,128)(2,1)S(1)}, bf16[32,16,64]{2,1,0:T(8,128)(2,1)}, u32[]{:S(2)}) copy-start(bf16[32,16,64]{2,1,0:T(8,128)(2,1)} %param.10) | copy-start | bytes 196612
  81.2 12.8 %copy-start.3 = (f32[64]{0:T(128)S(1)}, f32[64]{0:T(128)}, u32[]{:S(2)}) copy-start(f32[64]{0:T(128)} %param.12) | copy-start | bytes 772
  82.2 11.4 %all-to-all-start.2 = ((bf16[32,2,512]{2,1,0:T(2,128)(2,1)}), bf16[32,2,512]{2,1,0:T(2,128)(2,1)S(1)}, u32[]{:S(2)}, u32[]{:S(2)}) async-start(bf16[32,2,512]{2,1,0:T(2,128)(2,1)} %reshape.136), calls=%async_computation.2 | async-start | bytes 131072 | tf_op jit(solution)/shard_map/all_to_all | solution.py:64
  86.2 85.7 %all-gather.5.cloned.1.call-start = ((), (), s32[]{:S(2)}) async-start(), calls=%async_computation.5 | async-start | bytes 4325376 | tf_op jit(solution)/shard_map/all_gather | solution.py:104
  94.5 26.1 %copy-start.1 = (bf16[32,16,64]{2,1,0:T(8,128)(2,1)}, bf16[32,16,64]{2,1,0:T(8,128)(2,1)S(1)}, u32[]{:S(2)}) copy-start(bf16[32,16,64]{2,1,0:T(8,128)(2,1)S(1)} %copy.80) | copy-start | bytes 196612
  120.5 51.3 %copy-start.4 = (bf16[32,16,128]{2,1,0:T(8,128)(2,1)S(1)}, bf16[32,16,128]{2,1,0:T(8,128)(2,1)}, u32[]{:S(2)}) copy-start(bf16[32,16,128]{2,1,0:T(8,128)(2,1)} %param.13) | copy-start | bytes 393220
Sparse Core Ops, SparseCore 0:
  10.5 58.7 all-gather.2
  123.5 48.3 all-gather.4
